TPU v7x, 256 devices: a whole 4x4x8 slice. The times are simulated.
256 devices in a mesh: space: 32 (over x, z_hi, y), ens: 8 (over z_lo, core).
Axes of the slice: x: 4, y: 4, z: 8 (z_hi: 2, z_lo: 4; z = z_hi * 4 + z_lo), core: 2. Of those that a mesh axis runs over, the one named last changes fastest.
Arguments:
- outlook_array: bfloat16 [1536, 49152], P('ens', 'space'), may hold values from -57 to 57
- earlier_location_basis: bfloat16 [49152, 256], P('space'), may hold values from -4 to 4
- earlier_ensemble_basis: float32 [48, 16], replicated, may hold values from -4 to 4
- earlier_height_basis: float32 [32, 16], replicated, may hold values from -4 to 4
Outputs:
- spatial_factor: float32 [49152, 256], P(('space', 'ens'))
- member_factor: float32 [48, 16], replicated
- level_factor: float32 [32, 16], replicated
All inputs are finite; a program needn't handle non-finite values.
Results may differ from a plain program's by a relative error of at most 0.0075.
The roundings to bfloat16 on the way count: a program that leaves them out, or rounds other values in their place, can miss the bound.
Values may be sent and summed in bfloat16 or wider, within the bound.
A program may use at most 64 MiB of HBM per device.

v0:
```python
import jax
import jax.numpy as jnp
from jax import lax
from jax.sharding import PartitionSpec as P

MEMBERS = 48
LEVELS = 32
PASSES = 3
highest = lax.Precision.HIGHEST


def inner_gram(image_rows):
    return lax.dot_general(
        image_rows,
        image_rows,
        (((0,), (0,)), ((), ())),
        precision=highest,
        preferred_element_type=jnp.float32,
    )


def solve_right(lower_factor, image_rows):
    return lax.linalg.triangular_solve(
        lower_factor, image_rows, left_side=False, lower=True, transpose_a=True
    )


def refine(gram_matrix, previous, row_count):
    image_rows = jnp.dot(
        gram_matrix, previous, precision=highest, preferred_element_type=jnp.float32
    )
    lower_factor = jnp.linalg.cholesky(inner_gram(image_rows) / row_count)
    return solve_right(lower_factor, image_rows)


def factor_grams(final_band_lines):
    by_level = final_band_lines.reshape(LEVELS, -1)
    level_gram = jnp.dot(by_level, by_level.T, preferred_element_type=jnp.float32)
    by_member = (
        final_band_lines.reshape(LEVELS, MEMBERS, -1).transpose(1, 0, 2).reshape(MEMBERS, -1)
    )
    member_gram = jnp.dot(by_member, by_member.T, preferred_element_type=jnp.float32)
    return (member_gram, level_gram)


def spatial_step(ensemble_variance, grid_total):
    gram_total = lax.psum(inner_gram(ensemble_variance), ("space", "ens")) / grid_total
    return solve_right(jnp.linalg.cholesky(gram_total), ensemble_variance)


def project(vertical_cells, location_basis_matrix):
    row_share = lax.psum_scatter(
        jnp.dot(vertical_cells, location_basis_matrix, preferred_element_type=jnp.float32),
        "ens",
        scatter_dimension=0,
        tiled=True,
    )
    row_share = lax.psum(row_share, "space")
    return lax.all_gather(row_share.astype(jnp.bfloat16), "ens", axis=0, tiled=True)


def on_device(outlook_array, earlier_location_basis, earlier_ensemble_basis, earlier_height_basis):
    ens_count = lax.axis_size("ens")
    grid_dev = earlier_location_basis.shape[0]
    sub_rows = grid_dev // ens_count
    grid_total = grid_dev * lax.axis_size("space")
    factor = None
    final_band_lines = None
    vertical_cells = lax.all_to_all(outlook_array, "ens", split_axis=1, concat_axis=0, tiled=True)
    first_row = lax.axis_index("ens") * sub_rows
    location_basis_matrix = lax.dynamic_slice_in_dim(earlier_location_basis, first_row, sub_rows, 0)
    for pass_index in range(PASSES + 1):
        final_band_lines = project(vertical_cells, location_basis_matrix)
        if pass_index < PASSES:
            ensemble_variance = lax.dot_general(
                vertical_cells,
                final_band_lines,
                (((0,), (0,)), ((), ())),
                preferred_element_type=jnp.float32,
            )
            factor = spatial_step(ensemble_variance, grid_total)
            location_basis_matrix = factor.astype(jnp.bfloat16)
    member_gram, level_gram = factor_grams(final_band_lines)
    return (
        factor,
        refine(member_gram, earlier_ensemble_basis, MEMBERS),
        refine(level_gram, earlier_height_basis, LEVELS),
    )


def solution(mesh):
    in_specs = (P("ens", "space"), P("space", None), P(), P())
    out_specs = (P(("space", "ens"), None), P(), P())
    return jax.shard_map(
        on_device, mesh=mesh, in_specs=in_specs, out_specs=out_specs, check_vma=False
    )
```

profile of v0, /device:TPU:1, one launch (start us, length us, event | category | flops | bytes accessed | tf_op | source)
XLA Modules:
  0.0 2115.9 jit_solution(5704616628953250704)
XLA Ops:
  9.5 7.4 all-to-all-start
  16.9 20.0 all-to-all-done
  40.1 37.7 %reduce-scatter.13.cloned.1.call-done = f32[192,256]{1,0:T(8,128)} async-done(((f32[1536,256]{1,0:T(8,128)}), f32[192,256]{1,0:T(8,128)}) %reduce-scatter.13.cloned.1.call-update) | async-done | bytes 196624 | tf_op jit(solution)/shard_map/reduce_scatter | solution.py:52
  77.8 198.7 %all-reduce.14 = bf16[192,256]{1,0:T(8,128)(2,1)S(1)} all-reduce(f32[192,256]{1,0:T(8,128)} %reduce-scatter.13.cloned.1.call-done), channel_id=1, replica_groups=mesh['space'=32,'ens'=8] {'space'}, use_global_device_ids=true, to_apply=%region_1.0 | all-reduce | flops 49152 | bytes 294912 | tf_op jit(solution)/shard_map/psum | solution.py:58
  276.4 44.7 %all_gather.12 = bf16[1536,256]{1,0:T(8,128)(2,1)S(1)} all-gather(bf16[192,256]{1,0:T(8,128)(2,1)S(1)} %all-reduce.14), channel_id=1, replica_groups=mesh['space'=32,'ens'=8] {'ens'}, dimensions={0}, use_global_device_ids=true | all-gather | bytes 884736 | tf_op jit(solution)/shard_map/all_gather | solution.py:59
  323.4 243.8 %all-reduce.9.cloned.1.call-done = f32[256,256]{0,1:T(8,128)} async-done(((f32[256,256]{0,1:T(8,128)}), f32[256,256]{0,1:T(8,128)}) %all-reduce.9.cloned.1.call-update) | async-done | bytes 262160 | tf_op jit(solution)/shard_map/psum | solution.py:47
  569.3 11.7 cholesky.214
  581.1 9.8 custom-call.25
  591.4 11.7 cholesky.231
  605.3 4.3 while.6
  609.6 19.7 custom-call.26
  632.2 37.2 %reduce-scatter.15.cloned.1.call-done = f32[192,256]{1,0:T(8,128)} async-done(((f32[1536,256]{1,0:T(8,128)}), f32[192,256]{1,0:T(8,128)}) %reduce-scatter.15.cloned.1.call-update) | async-done | bytes 196624 | tf_op jit(solution)/shard_map/reduce_scatter | solution.py:52
  669.3 198.6 %all-reduce.15 = bf16[192,256]{1,0:T(8,128)(2,1)S(1)} all-reduce(f32[192,256]{1,0:T(8,128)} %reduce-scatter.15.cloned.1.call-done), channel_id=1, replica_groups=mesh['space'=32,'ens'=8] {'space'}, use_global_device_ids=true, to_apply=%region_8.11 | all-reduce | flops 49152 | bytes 294912 | tf_op jit(solution)/shard_map/psum | solution.py:58
  867.9 44.7 %all_gather.13 = bf16[1536,256]{1,0:T(8,128)(2,1)S(1)} all-gather(bf16[192,256]{1,0:T(8,128)(2,1)S(1)} %all-reduce.15), channel_id=1, replica_groups=mesh['space'=32,'ens'=8] {'ens'}, dimensions={0}, use_global_device_ids=true | all-gather | bytes 884736 | tf_op jit(solution)/shard_map/all_gather | solution.py:59
  914.4 244.5 %all-reduce.11.cloned.1.call-done = f32[256,256]{0,1:T(8,128)} async-done(((f32[256,256]{0,1:T(8,128)}), f32[256,256]{0,1:T(8,128)}) %all-reduce.11.cloned.1.call-update) | async-done | bytes 262160 | tf_op jit(solution)/shard_map/psum | solution.py:47
  1161.1 11.7 cholesky.248
  1172.8 9.8 custom-call.27
  1183.1 11.7 cholesky.265
  1197.6 4.5 while.7
  1202.1 19.7 custom-call.28
  1224.7 37.2 %reduce-scatter.17.cloned.1.call-done = f32[192,256]{1,0:T(8,128)} async-done(((f32[1536,256]{1,0:T(8,128)}), f32[192,256]{1,0:T(8,128)}) %reduce-scatter.17.cloned.1.call-update) | async-done | bytes 196624 | tf_op jit(solution)/shard_map/reduce_scatter | solution.py:52
  1261.9 198.8 %all-reduce.16 = bf16[192,256]{1,0:T(8,128)(2,1)S(1)} all-reduce(f32[192,256]{1,0:T(8,128)} %reduce-scatter.17.cloned.1.call-done), channel_id=1, replica_groups=mesh['space'=32,'ens'=8] {'space'}, use_global_device_ids=true, to_apply=%region_11.14 | all-reduce | flops 49152 | bytes 294912 | tf_op jit(solution)/shard_map/psum | solution.py:58
  1460.7 44.6 %all_gather.14 = bf16[1536,256]{1,0:T(8,128)(2,1)S(1)} all-gather(bf16[192,256]{1,0:T(8,128)(2,1)S(1)} %all-reduce.16), channel_id=1, replica_groups=mesh['space'=32,'ens'=8] {'ens'}, dimensions={0}, use_global_device_ids=true | all-gather | bytes 884736 | tf_op jit(solution)/shard_map/all_gather | solution.py:59
  1507.1 244.3 %all-reduce.13.cloned.1.call-done = f32[256,256]{0,1:T(8,128)} async-done(((f32[256,256]{0,1:T(8,128)}), f32[256,256]{0,1:T(8,128)}) %all-reduce.13.cloned.1.call-update) | async-done | bytes 262160 | tf_op jit(solution)/shard_map/psum | solution.py:47
  1753.5 11.7 cholesky.282
  1765.3 9.8 custom-call.29
  1775.6 11.7 cholesky.299
  1790.0 4.2 while.8
  1794.2 19.7 custom-call.30
  1816.7 37.2 %reduce-scatter.19.cloned.1.call-done = f32[192,256]{1,0:T(8,128)} async-done(((f32[1536,256]{1,0:T(8,128)}), f32[192,256]{1,0:T(8,128)}) %reduce-scatter.19.cloned.1.call-update) | async-done | bytes 196624 | tf_op jit(solution)/shard_map/reduce_scatter | solution.py:52
  1853.9 198.8 %all-reduce.17 = bf16[192,256]{1,0:T(8,128)(2,1)S(1)} all-reduce(f32[192,256]{1,0:T(8,128)} %reduce-scatter.19.cloned.1.call-done), channel_id=1, replica_groups=mesh['space'=32,'ens'=8] {'space'}, use_global_device_ids=true, to_apply=%region_14.17 | all-reduce | flops 49152 | bytes 294912 | tf_op jit(solution)/shard_map/psum | solution.py:58
  2052.7 44.6 %all_gather.15 = bf16[1536,256]{1,0:T(8,128)(2,1)S(1)} all-gather(bf16[192,256]{1,0:T(8,128)(2,1)S(1)} %all-reduce.17), channel_id=1, replica_groups=mesh['space'=32,'ens'=8] {'ens'}, dimensions={0}, use_global_device_ids=true | all-gather | bytes 884736 | tf_op jit(solution)/shard_map/all_gather | solution.py:59
  (130 shorter events, 54.7 us)
Async XLA Ops:
  7.2 30.8 %copy-start = (bf16[1536,256]{1,0:T(8,128)(2,1)S(1)}, bf16[1536,256]{1,0:T(8,128)(2,1)}, u32[]{:S(2)}) copy-start(bf16[1536,256]{1,0:T(8,128)(2,1)} %param.9) | copy-start | bytes 2359300
  9.5 27.4 %all-to-all-start = ((bf16[192,8,192]{0,2,1:T(8,128)(2,1)}), bf16[192,8,192]{0,2,1:T(8,128)(2,1)S(1)}, u32[]{:S(2)}, u32[]{:S(2)}) async-start(bf16[192,8,192]{0,2,1:T(8,128)(2,1)} %bitcast), calls=%async_computation | async-start | bytes 1572864 | tf_op jit(solution)/shard_map/all_to_all | solution.py:69
  16.9 60.9 %reduce-scatter.13.cloned.1.call-start = ((), (), s32[]{:S(2)}) async-start(), calls=%async_computation.8 | async-start | bytes 1769472 | tf_op jit(solution)/shard_map/reduce_scatter | solution.py:52
  40.0 527.2 %all-reduce.9.cloned.1.call-start = ((), (), s32[]{:S(2)}) async-start(), calls=%async_computation.5 | async-start | bytes 524288 | tf_op jit(solution)/shard_map/psum | solution.py:47
  322.8 346.5 %reduce-scatter.15.cloned.1.call-start = ((), (), s32[]{:S(2)}) async-start(), calls=%async_computation.9 | async-start | bytes 1769472 | tf_op jit(solution)/shard_map/reduce_scatter | solution.py:52
  632.1 526.8 %all-reduce.11.cloned.1.call-start = ((), (), s32[]{:S(2)}) async-start(), calls=%async_computation.6 | async-start | bytes 524288 | tf_op jit(solution)/shard_map/psum | solution.py:47
  914.3 347.6 %reduce-scatter.17.cloned.1.call-start = ((), (), s32[]{:S(2)}) async-start(), calls=%async_computation.10 | async-start | bytes 1769472 | tf_op jit(solution)/shard_map/reduce_scatter | solution.py:52
  1224.6 526.8 %all-reduce.13.cloned.1.call-start = ((), (), s32[]{:S(2)}) async-start(), calls=%async_computation.7 | async-start | bytes 524288 | tf_op jit(solution)/shard_map/psum | solution.py:47
  1507.1 346.9 %reduce-scatter.19.cloned.1.call-start = ((), (), s32[]{:S(2)}) async-start(), calls=%async_computation.11 | async-start | bytes 1769472 | tf_op jit(solution)/shard_map/reduce_scatter | solution.py:52
  1814.6 2.0 copy-start.1
  2097.3 0.7 copy-start.3
  2097.7 5.9 copy-start.2
Sparse Core Ops, SparseCore 0:
  40.1 37.5 reduce-scatter.12
  323.0 244.1 all-reduce.8
  632.2 37.0 reduce-scatter.14
  914.5 244.4 all-reduce.10
  1224.8 37.0 reduce-scatter.16
  1507.2 244.1 all-reduce.12
  1816.8 37.0 reduce-scatter.18
where the time goes:
time: 2120 us
  blocking collectives  973 us (46%)
  waiting for transfers between devices  902 us (43%)
  other arithmetic  176 us (8%)
  local copies, waits for them, and re-layouts  23.1 us (1%)
    psum x4, blocking collectives, project(): row_share = lax.psum(row_share, 'space')  795 us
    psum x3, waiting for transfers between devices, spatial_step(): lax.psum(inner_gram(ensemble_variance), ('space', 'ens')) / grid_total  733 us
    all_gather x4, blocking collectives, project(): lax.all_gather(row_share.astype(jnp.bfloat16), 'ens', axis=0, tiled=True)  179 us
    reduce_scatter x4, waiting for transfers between devices, project(): lax.psum_scatter(jnp.dot(vertical_cells, location_basis_matrix, preferred...  149 us
    another operation x20, other arithmetic, spatial_step(): return solve_right(jnp.linalg.cholesky(gram_total), ensemble_variance)  103 us
    another operation x12, other arithmetic, solve_right(): lax.linalg.triangular_solve(lower_factor, image_rows, left_side=False, lo...  62.9 us
  transfers between devices with their start and end apart: 8, of which 8 were waited for; matrix products, arithmetic and copies ran while one was open for 0% of the time, Pallas kernels for 0%

commit v1 on v0

--- a/solution.py
+++ b/solution.py
@@ -55,7 +55,7 @@
         scatter_dimension=0,
         tiled=True,
     )
-    row_share = lax.psum(row_share, "space")
+    row_share = jnp.sum(lax.all_gather(row_share, "space"), axis=0)
     return lax.all_gather(row_share.astype(jnp.bfloat16), "ens", axis=0, tiled=True)
 
 

time: 2120 us -> 1780 us (0.84)
  blocking collectives: 973 us -> 69.7 us
  waiting for transfers between devices: 902 us -> 1450 us
    psum x4 -> x0, blocking collectives: 795 us -> none  [project(): row_share = lax.psum(row_share, 'space')]
    all_gather x0 -> x4, waiting for transfers between devices: none -> 542 us  [project(): row_share = jnp.sum(lax.all_gather(row_share, 'space'), axis=0)]
    all_gather x4, blocking collectives: 179 us -> 69.7 us  [project(): lax.all_gather(row_share.astype(jnp.bfloat16), 'ens', axis=0, tiled=True)]
  transfers between devices with their start and end apart: 8 -> 12, of which waited for: 8 -> 12; matrix products, arithmetic and copies ran while one was open for 0% -> 0% of each run, Pallas kernels for 0% -> 0%
where the time goes in v1:
time: 1780 us; the launch traced here: 1770 us
  waiting for transfers between devices  1450 us (81%)
  other arithmetic  189 us (11%)
  blocking collectives  69.7 us (4%)
  local copies, waits for them, and re-layouts  23.1 us (1%)
  between operations  18.5 us (1%)
    psum x3, waiting for transfers between devices, spatial_step(): lax.psum(inner_gram(ensemble_variance), ('space', 'ens')) / grid_total  740 us
    all_gather x4, waiting for transfers between devices, project(): row_share = jnp.sum(lax.all_gather(row_share, 'space'), axis=0)  542 us
    reduce_scatter x4, waiting for transfers between devices, project(): lax.psum_scatter(jnp.dot(vertical_cells, location_basis_matrix, preferred...  149 us
    another operation x20, other arithmetic, spatial_step(): return solve_right(jnp.linalg.cholesky(gram_total), ensemble_variance)  103 us
    all_gather x4, blocking collectives, project(): lax.all_gather(row_share.astype(jnp.bfloat16), 'ens', axis=0, tiled=True)  69.7 us
    another operation x12, other arithmetic, solve_right(): lax.linalg.triangular_solve(lower_factor, image_rows, left_side=False, lo...  62.9 us
  transfers between devices with their start and end apart: 12, of which 12 were waited for; matrix products, arithmetic and copies ran while one was open for 0% of the time, Pallas kernels for 0%

profile of v1, /device:TPU:1, one launch (start us, length us, event | category | flops | bytes accessed | tf_op | source)
XLA Modules:
  0.0 1774.1 jit_solution(1929490882614571627)
XLA Ops:
  9.5 7.4 all-to-all-start
  16.9 20.0 %all-to-all-done = bf16[192,8,192]{0,2,1:T(8,128)(2,1)S(1)} async-done(((bf16[192,8,192]{0,2,1:T(8,128)(2,1)}), bf16[192,8,192]{0,2,1:T(8,128)(2,1)S(1)}, u32[]{:S(2)}, u32[]{:S(2)}) %all-to-all-start) | async-done | bytes 589856 | tf_op jit(solution)/shard_map/all_to_all | solution.py:69
  40.1 37.7 %reduce-scatter.13.cloned.1.call-done = f32[192,256]{1,0:T(8,128)} async-done(((f32[1536,256]{1,0:T(8,128)}), f32[192,256]{1,0:T(8,128)}) %reduce-scatter.13.cloned.1.call-update) | async-done | bytes 196624 | tf_op jit(solution)/shard_map/reduce_scatter | solution.py:52
  77.8 135.7 %all-gather.9.cloned.1.call-done = f32[6144,256]{1,0:T(8,128)} async-done(((f32[192,256]{1,0:T(8,128)}), f32[6144,256]{1,0:T(8,128)}) %all-gather.9.cloned.1.call-update) | async-done | bytes 6291472 | tf_op jit(solution)/shard_map/all_gather | solution.py:58
  216.7 17.4 all_gather.38
  236.1 246.3 %all-reduce.5.cloned.1.call-done = f32[256,256]{0,1:T(8,128)} async-done(((f32[256,256]{0,1:T(8,128)}), f32[256,256]{0,1:T(8,128)}) %all-reduce.5.cloned.1.call-update) | async-done | bytes 262160 | tf_op jit(solution)/shard_map/psum | solution.py:47
  484.6 11.7 cholesky.214
  496.3 9.8 custom-call.25
  506.6 11.7 cholesky.231
  520.6 4.5 while.6
  525.1 19.7 %custom-call.26 = f32[2,128,128]{1,2,0:T(8,128)S(1)} custom-call(f32[2,128,128]{2,1,0:T(8,128)S(1)} %get-tuple-element.26), custom_call_target="InvertDiagBlocksLowerTriangular" | custom-call | tf_op jit(solution)/shard_map/triangular_solve/custom-call.4 | solution.py:23
  547.6 37.2 %reduce-scatter.15.cloned.1.call-done = f32[192,256]{1,0:T(8,128)} async-done(((f32[1536,256]{1,0:T(8,128)}), f32[192,256]{1,0:T(8,128)}) %reduce-scatter.15.cloned.1.call-update) | async-done | bytes 196624 | tf_op jit(solution)/shard_map/reduce_scatter | solution.py:52
  584.9 135.4 %all-gather.11.cloned.1.call-done = f32[6144,256]{1,0:T(8,128)} async-done(((f32[192,256]{1,0:T(8,128)}), f32[6144,256]{1,0:T(8,128)}) %all-gather.11.cloned.1.call-update) | async-done | bytes 6291472 | tf_op jit(solution)/shard_map/all_gather | solution.py:58
  723.5 17.4 all_gather.41
  742.7 246.7 %all-reduce.7.cloned.1.call-done = f32[256,256]{0,1:T(8,128)} async-done(((f32[256,256]{0,1:T(8,128)}), f32[256,256]{0,1:T(8,128)}) %all-reduce.7.cloned.1.call-update) | async-done | bytes 262160 | tf_op jit(solution)/shard_map/psum | solution.py:47
  991.6 11.7 cholesky.248
  1003.4 9.8 custom-call.27
  1013.7 11.7 cholesky.265
  1028.2 4.3 while.7
  1032.4 19.7 %custom-call.28 = f32[2,128,128]{1,2,0:T(8,128)S(1)} custom-call(f32[2,128,128]{2,1,0:T(8,128)S(1)} %get-tuple-element.27), custom_call_target="InvertDiagBlocksLowerTriangular" | custom-call | tf_op jit(solution)/shard_map/triangular_solve/custom-call.4 | solution.py:23
  1055.0 37.2 %reduce-scatter.17.cloned.1.call-done = f32[192,256]{1,0:T(8,128)} async-done(((f32[1536,256]{1,0:T(8,128)}), f32[192,256]{1,0:T(8,128)}) %reduce-scatter.17.cloned.1.call-update) | async-done | bytes 196624 | tf_op jit(solution)/shard_map/reduce_scatter | solution.py:52
  1092.3 135.6 %all-gather.13.cloned.1.call-done = f32[6144,256]{1,0:T(8,128)} async-done(((f32[192,256]{1,0:T(8,128)}), f32[6144,256]{1,0:T(8,128)}) %all-gather.13.cloned.1.call-update) | async-done | bytes 6291472 | tf_op jit(solution)/shard_map/all_gather | solution.py:58
  1231.0 17.4 all_gather.44
  1250.3 246.7 %all-reduce.9.cloned.1.call-done = f32[256,256]{0,1:T(8,128)} async-done(((f32[256,256]{0,1:T(8,128)}), f32[256,256]{0,1:T(8,128)}) %all-reduce.9.cloned.1.call-update) | async-done | bytes 262160 | tf_op jit(solution)/shard_map/psum | solution.py:47
  1499.1 11.7 cholesky.282
  1510.9 9.8 custom-call.29
  1521.2 11.7 cholesky.299
  1535.5 4.2 while.8
  1539.8 19.7 %custom-call.30 = f32[2,128,128]{1,2,0:T(8,128)S(1)} custom-call(f32[2,128,128]{2,1,0:T(8,128)S(1)} %get-tuple-element.28), custom_call_target="InvertDiagBlocksLowerTriangular" | custom-call | tf_op jit(solution)/shard_map/triangular_solve/custom-call.4 | solution.py:23
  1562.3 37.2 %reduce-scatter.19.cloned.1.call-done = f32[192,256]{1,0:T(8,128)} async-done(((f32[1536,256]{1,0:T(8,128)}), f32[192,256]{1,0:T(8,128)}) %reduce-scatter.19.cloned.1.call-update) | async-done | bytes 196624 | tf_op jit(solution)/shard_map/reduce_scatter | solution.py:52
  1599.6 135.6 %all-gather.15.cloned.1.call-done = f32[6144,256]{1,0:T(8,128)} async-done(((f32[192,256]{1,0:T(8,128)}), f32[6144,256]{1,0:T(8,128)}) %all-gather.15.cloned.1.call-update) | async-done | bytes 6291472 | tf_op jit(solution)/shard_map/all_gather | solution.py:58
  1738.4 17.4 all_gather.47
  (142 shorter events, 67.3 us)
Async XLA Ops:
  7.2 30.8 %copy-start = (bf16[1536,256]{1,0:T(8,128)(2,1)S(1)}, bf16[1536,256]{1,0:T(8,128)(2,1)}, u32[]{:S(2)}) copy-start(bf16[1536,256]{1,0:T(8,128)(2,1)} %param.9) | copy-start | bytes 2359300
  9.5 27.4 %all-to-all-start = ((bf16[192,8,192]{0,2,1:T(8,128)(2,1)}), bf16[192,8,192]{0,2,1:T(8,128)(2,1)S(1)}, u32[]{:S(2)}, u32[]{:S(2)}) async-start(bf16[192,8,192]{0,2,1:T(8,128)(2,1)} %bitcast), calls=%async_computation | async-start | bytes 1572864 | tf_op jit(solution)/shard_map/all_to_all | solution.py:69
  16.9 60.9 %reduce-scatter.13.cloned.1.call-start = ((), (), s32[]{:S(2)}) async-start(), calls=%async_computation.12 | async-start | bytes 1769472 | tf_op jit(solution)/shard_map/reduce_scatter | solution.py:52
  40.0 173.5 %all-gather.9.cloned.1.call-start = ((), (), s32[]{:S(2)}) async-start(), calls=%async_computation.8 | async-start | bytes 6488064 | tf_op jit(solution)/shard_map/all_gather | solution.py:58
  77.8 404.7 %all-reduce.5.cloned.1.call-start = ((), (), s32[]{:S(2)}) async-start(), calls=%async_computation.5 | async-start | bytes 524288 | tf_op jit(solution)/shard_map/psum | solution.py:47
  235.9 349.0 %reduce-scatter.15.cloned.1.call-start = ((), (), s32[]{:S(2)}) async-start(), calls=%async_computation.13 | async-start | bytes 1769472 | tf_op jit(solution)/shard_map/reduce_scatter | solution.py:52
  547.6 172.8 %all-gather.11.cloned.1.call-start = ((), (), s32[]{:S(2)}) async-start(), calls=%async_computation.9 | async-start | bytes 6488064 | tf_op jit(solution)/shard_map/all_gather | solution.py:58
  584.9 404.6 %all-reduce.7.cloned.1.call-start = ((), (), s32[]{:S(2)}) async-start(), calls=%async_computation.6 | async-start | bytes 524288 | tf_op jit(solution)/shard_map/psum | solution.py:47
  742.7 349.5 %reduce-scatter.17.cloned.1.call-start = ((), (), s32[]{:S(2)}) async-start(), calls=%async_computation.14 | async-start | bytes 1769472 | tf_op jit(solution)/shard_map/reduce_scatter | solution.py:52
  1054.9 172.9 %all-gather.13.cloned.1.call-start = ((), (), s32[]{:S(2)}) async-start(), calls=%async_computation.10 | async-start | bytes 6488064 | tf_op jit(solution)/shard_map/all_gather | solution.py:58
  1092.2 404.8 %all-reduce.9.cloned.1.call-start = ((), (), s32[]{:S(2)}) async-start(), calls=%async_computation.7 | async-start | bytes 524288 | tf_op jit(solution)/shard_map/psum | solution.py:47
  1250.2 349.3 %reduce-scatter.19.cloned.1.call-start = ((), (), s32[]{:S(2)}) async-start(), calls=%async_computation.15 | async-start | bytes 1769472 | tf_op jit(solution)/shard_map/reduce_scatter | solution.py:52
  1560.2 2.0 copy-start.1
  1562.3 172.9 %all-gather.15.cloned.1.call-start = ((), (), s32[]{:S(2)}) async-start(), calls=%async_computation.11 | async-start | bytes 6488064 | tf_op jit(solution)/shard_map/all_gather | solution.py:58
  1755.8 0.7 copy-start.3
  1756.2 5.9 copy-start.2
Sparse Core Ops, SparseCore 0:
  40.1 37.5 reduce-scatter.12
  81.1 132.3 all-gather.8
  236.0 246.4 all-reduce.4
  547.7 37.0 reduce-scatter.14
  588.1 132.2 all-gather.10
  742.8 246.6 all-reduce.6
  1055.1 37.0 reduce-scatter.16
  1095.6 132.2 all-gather.12
  1250.3 246.6 all-reduce.8
  1562.4 37.0 reduce-scatter.18
  1602.9 132.2 all-gather.14
